TPU v7x, 256 devices: a whole 4x4x8 slice. The times are simulated.
256 devices in a mesh: dp: 2 (over y_lo), ulysses: 8 (over x, core), blk: 16 (over y_hi, z).
Axes of the slice: x: 4, y: 4 (y_hi: 2, y_lo: 2; y = y_hi * 2 + y_lo), z: 8, core: 2. Of those that a mesh axis runs over, the one named last changes fastest.
Arguments:
- hidden_in: bfloat16 [2, 16384, 4096], P('dp', ('blk', 'ulysses')), may hold values from -6 to 6
- queries: bfloat16 [2, 16384, 2048], P('dp', ('blk', 'ulysses')), may hold values from -240 to 240
- pair_weight: bfloat16 [4096, 2048], P(('dp', 'blk')), may hold values from -0.09375 to 0.09375
- span_order: int32 [2, 32], P('dp'), may hold values from 0 to 31, each once within a row
- yarn_divisor: int32 [64], replicated, may hold values from 1 to 8
Outputs:
- attended: bfloat16 [2, 16384, 2048], P('dp', ('blk', 'ulysses'))
All inputs are finite; a program needn't handle non-finite values.
Results may differ from a plain program's by a relative error of at most 0.02.
The roundings to bfloat16 on the way count: a program that leaves them out, or rounds other values in their place, can miss the bound.
Values may be sent and summed in bfloat16 or wider, within the bound.
A program may use at most 128 MiB of HBM per device.

v0:
```python
import math
import jax
import jax.numpy as jnp
from jax import lax
from jax.sharding import PartitionSpec as P

KVH = 8
HD = 128
QH = 16
STEPS = 3
LOG_BASE = math.log(500000.0)


def from_behind(block, axis, distance):
    devices = range(lax.axis_size(axis))
    route = [((i - distance) % len(devices), i) for i in devices]
    return lax.ppermute(block, axis, route)


def rotate(vectors, angle_table):
    half_dim = vectors.shape[-1] // 2
    first_half = vectors[..., :half_dim]
    second_half = vectors[..., half_dim:]
    cosine = jnp.cos(angle_table)
    sine_part = jnp.sin(angle_table)
    return jnp.concatenate(
        [
            first_half * cosine - second_half * sine_part,
            second_half * cosine + first_half * sine_part,
        ],
        axis=-1,
    )


def angles(positions, yarn_divisor):
    half_dim = yarn_divisor.shape[0]
    scaled = 2.0 * jnp.arange(half_dim, dtype=jnp.float32) / (2 * half_dim)
    inverse = jnp.exp(-LOG_BASE * scaled) / yarn_divisor.astype(jnp.float32)
    return positions.astype(jnp.float32)[:, None] * inverse[None, :]


def positions_of(order_row, first_row, row_count, span_rows):
    stored = first_row + jnp.arange(row_count, dtype=jnp.int32)
    span_index = stored // span_rows
    matches = span_index[:, None] == jnp.arange(order_row.shape[0], dtype=jnp.int32)[None, :]
    span_value = jnp.sum(jnp.where(matches, order_row[None, :], 0), axis=1)
    return span_value * span_rows + stored % span_rows


def tile_scores(query_rows, key_rows):
    product = lax.dot_general(
        query_rows, key_rows, (((1,), (1,)), ((), ())), preferred_element_type=jnp.float32
    )
    return product * (1.0 / math.sqrt(HD))


def row_maximum(query_rows, query_pos, key_rows, key_pos):
    score = tile_scores(query_rows, key_rows)
    return jnp.max(jnp.where(key_pos[None, :] <= query_pos[:, None], score, -jnp.inf), axis=1)


def add_tile(denominator, numerator, query_rows, query_pos, key_rows, value_rows, key_pos, row_top):
    score = tile_scores(query_rows, key_rows)
    allowed = key_pos[None, :] <= query_pos[:, None]
    weights = jnp.where(allowed, jnp.exp(score - row_top[:, None]), 0.0)
    denominator = denominator + jnp.sum(weights, axis=1)
    numerator = numerator + jnp.dot(
        weights.astype(jnp.bfloat16), value_rows, preferred_element_type=jnp.float32
    )
    return (denominator, numerator)


def shards(hidden_in, queries, pair_weight, span_order, yarn_divisor):
    inputs_local = hidden_in[0]
    queries_local = queries[0]
    order_row = span_order[0]
    token_rows = inputs_local.shape[0]
    ulysses_size = lax.axis_size("ulysses")
    cycle_size = lax.axis_size("blk")
    ulysses_index = lax.axis_index("ulysses")
    cycle_index = lax.axis_index("blk")
    block_rows = token_rows * ulysses_size
    span_rows = block_rows // 2
    kv_width = KVH * HD
    group_size = QH // KVH
    own_positions = positions_of(
        order_row, cycle_index * block_rows + ulysses_index * token_rows, token_rows, span_rows
    )
    own_angles = angles(own_positions, yarn_divisor)
    block_positions = positions_of(order_row, cycle_index * block_rows, block_rows, span_rows)
    rotated_queries = rotate(
        queries_local.astype(jnp.float32).reshape(token_rows, QH, HD), own_angles[:, None, :]
    )
    rotated_queries = rotated_queries.astype(jnp.bfloat16).reshape(token_rows, QH * HD)
    projected = jnp.dot(
        inputs_local,
        lax.all_gather(pair_weight, ("dp", "blk"), axis=0, tiled=True),
        preferred_element_type=jnp.float32,
    )
    token_keys = rotate(
        projected[:, :kv_width].reshape(token_rows, KVH, HD), own_angles[:, None, :]
    )
    token_keys = token_keys.astype(jnp.bfloat16).reshape(token_rows, kv_width)
    token_values = projected[:, kv_width:].astype(jnp.bfloat16)
    query_block, key_block, value_block = (
        lax.all_to_all(rotated_queries, "ulysses", split_axis=1, concat_axis=0, tiled=True),
        lax.all_to_all(token_keys, "ulysses", split_axis=1, concat_axis=0, tiled=True),
        lax.all_to_all(token_values, "ulysses", split_axis=1, concat_axis=0, tiled=True),
    )
    own_pair = jnp.stack([key_block, value_block])
    carried_blocks = [own_pair]
    current_pair = own_pair
    for step_index in range(STEPS):
        current_pair = from_behind(current_pair, "blk", 1)
        carried_blocks.append(current_pair)
    carried_positions = []
    for step_index in range(STEPS + 1):
        source_block = jnp.remainder(cycle_index - step_index, cycle_size)
        carried_positions.append(
            positions_of(order_row, source_block * block_rows, block_rows, span_rows)
        )
    output_rows = []
    for query_half in range(2):
        row_start = query_half * span_rows
        half_positions = block_positions[row_start : row_start + span_rows]
        query_pos = jnp.tile(half_positions, group_size)
        query_part = query_block[row_start : row_start + span_rows, 0 : group_size * HD]
        query_rows = (
            query_part.reshape(span_rows, group_size, HD)
            .transpose(1, 0, 2)
            .reshape(group_size * span_rows, HD)
        )
        tile_list = []
        for step_index in range(STEPS + 1):
            pair_block = carried_blocks[step_index]
            for key_half in range(2):
                key_start = key_half * span_rows
                key_rows = pair_block[0, key_start : key_start + span_rows, 0:HD]
                value_rows = pair_block[1, key_start : key_start + span_rows, 0:HD]
                key_pos = carried_positions[step_index][key_start : key_start + span_rows]
                tile_list.append((key_rows, value_rows, key_pos))
        row_top = jnp.full((group_size * span_rows,), -jnp.inf, jnp.float32)
        for key_rows, value_rows, key_pos in tile_list:
            tile_top = row_maximum(query_rows, query_pos, key_rows, key_pos)
            row_top = jnp.maximum(row_top, tile_top)
        denominator = jnp.zeros((group_size * span_rows,), jnp.float32)
        numerator = jnp.zeros((group_size * span_rows, HD), jnp.float32)
        for key_rows, value_rows, key_pos in tile_list:
            denominator, numerator = add_tile(
                denominator,
                numerator,
                query_rows,
                query_pos,
                key_rows,
                value_rows,
                key_pos,
                row_top,
            )
        normalized = (numerator / denominator[:, None]).astype(jnp.bfloat16)
        normalized = (
            normalized.reshape(group_size, span_rows, HD)
            .transpose(1, 0, 2)
            .reshape(span_rows, group_size * HD)
        )
        output_rows.append(normalized)
    block_output = jnp.concatenate(output_rows, axis=0)
    token_output = lax.all_to_all(block_output, "ulysses", split_axis=0, concat_axis=1, tiled=True)
    return token_output[None]


def solution(mesh):
    return jax.shard_map(
        shards,
        mesh=mesh,
        in_specs=(
            P("dp", ("blk", "ulysses"), None),
            P("dp", ("blk", "ulysses"), None),
            P(("dp", "blk"), None),
            P("dp", None),
            P(),
        ),
        out_specs=P("dp", ("blk", "ulysses"), None),
        check_vma=False,
    )
```

profile of v0, /device:TPU:1, one launch (start us, length us, event | category | flops | bytes accessed | tf_op | source)
XLA Modules:
  0.0 342.1 jit_solution(7863774611345590729)
XLA Ops:
  6.5 0.7 all-gather.2.cloned.1.call-update
  7.3 1.2 copy.29
  8.7 0.2 multiply_cosine_fusion
  8.9 0.2 subtract_convert_fusion.1
  9.0 0.8 pad_maximum_fusion
  9.9 6.6 %all-to-all-start = ((bf16[128,8,256]{0,2,1:T(8,128)(2,1)}), bf16[128,8,256]{0,2,1:T(8,128)(2,1)S(1)}, u32[]{:S(2)}, u32[]{:S(2)}) async-start(bf16[128,8,256]{0,2,1:T(8,128)(2,1)} %bitcast.2), calls=%async_computation | async-start | bytes 1048576 | tf_op jit(solution)/shard_map/all_to_all | solution.py:106
  16.8 0.2 select_reduce_fusion.4
  17.1 188.4 %all-gather.2.cloned.1.call-done = bf16[4096,2048]{1,0:T(8,128)(2,1)} async-done(((bf16[128,2048]{1,0:T(8,128)(2,1)}), bf16[4096,2048]{1,0:T(8,128)(2,1)}) %all-gather.2.cloned.1.call-update) | async-done | bytes 16777232 | tf_op jit(solution)/shard_map/all_gather | solution.py:97
  205.5 8.1 %fusion.58 = f32[128,2048]{1,0:T(8,128)S(1)} fusion(bf16[4096,2048]{1,0:T(8,128)(2,1)} %all-gather.2.cloned.1.call-done, bf16[1,128,4096]{2,1,0:T(8,128)(2,1)S(1)} %copy-done), kind=kOutput, calls=%fused_computation.98 | convolution fusion | flops 2147483648 | bytes 18874368 | tf_op jit(solution)/shard_map/dot_general | solution.py:95
  213.8 0.2 fusion.206
  214.0 0.2 subtract_convert_fusion
  214.2 0.8 pad_maximum_fusion.3
  215.0 5.1 %all-to-all-start.1 = ((bf16[128,8,128]{2,0,1:T(8,128)(2,1)}), bf16[128,8,128]{2,0,1:T(8,128)(2,1)S(1)}, u32[]{:S(2)}, u32[]{:S(2)}) async-start(bf16[128,8,128]{2,0,1:T(8,128)(2,1)} %pad_maximum_fusion.3), calls=%async_computation.1 | async-start | bytes 524288 | tf_op jit(solution)/shard_map/all_to_all | solution.py:107
  220.1 0.7 copy_bitcast_fusion
  220.9 5.7 %all-to-all-done.1 = bf16[128,8,128]{2,0,1:T(8,128)(2,1)S(1)} async-done(((bf16[128,8,128]{2,0,1:T(8,128)(2,1)}), bf16[128,8,128]{2,0,1:T(8,128)(2,1)S(1)}, u32[]{:S(2)}, u32[]{:S(2)}) %all-to-all-start.1) | async-done | bytes 262176 | tf_op jit(solution)/shard_map/all_to_all | solution.py:107
  226.6 4.4 %all-to-all-start.2 = ((bf16[128,8,128]{2,0,1:T(8,128)(2,1)}), bf16[128,8,128]{2,0,1:T(8,128)(2,1)S(1)}, u32[]{:S(2)}, u32[]{:S(2)}) async-start(bf16[128,8,128]{2,0,1:T(8,128)(2,1)} %copy_bitcast_fusion), calls=%async_computation.2 | async-start | bytes 524288 | tf_op jit(solution)/shard_map/all_to_all | solution.py:108
  231.0 0.1 copy.30
  231.5 5.9 %all-to-all-done.2 = bf16[128,8,128]{2,0,1:T(8,128)(2,1)S(1)} async-done(((bf16[128,8,128]{2,0,1:T(8,128)(2,1)}), bf16[128,8,128]{2,0,1:T(8,128)(2,1)S(1)}, u32[]{:S(2)}, u32[]{:S(2)}) %all-to-all-start.2) | async-done | bytes 262176 | tf_op jit(solution)/shard_map/all_to_all | solution.py:108
  237.6 0.4 fusion.126
  238.0 1.8 fusion.125
  239.8 13.8 %collective-permute-done = bf16[2,1024,128]{2,1,0:T(8,128)(2,1)S(1)} collective-permute-done((bf16[2,1024,128]{2,1,0:T(8,128)(2,1)S(1)}, bf16[2,1024,128]{2,1,0:T(8,128)(2,1)S(1)}, u32[]{:S(2)}, u32[]{:S(2)}) %collective-permute-start) | collective-permute-done | bytes 524320 | tf_op jit(solution)/shard_map/ppermute | solution.py:17
  253.6 0.4 fusion.130
  254.1 0.4 fusion.132
  254.5 1.7 fusion.131
  256.3 0.4 fusion.129
  256.7 12.2 %collective-permute-done.1 = bf16[2,1024,128]{2,1,0:T(8,128)(2,1)S(1)} collective-permute-done((bf16[2,1024,128]{2,1,0:T(8,128)(2,1)S(1)}, bf16[2,1024,128]{2,1,0:T(8,128)(2,1)S(1)}, u32[]{:S(2)}, u32[]{:S(2)}) %collective-permute-start.1) | collective-permute-done | bytes 524320 | tf_op jit(solution)/shard_map/ppermute | solution.py:17
  268.8 0.4 fusion.134
  269.3 0.4 fusion.136
  269.7 1.8 fusion.133
  271.5 1.8 fusion.135
  273.3 9.9 %collective-permute-done.2 = bf16[2,1024,128]{2,1,0:T(8,128)(2,1)S(1)} collective-permute-done((bf16[2,1024,128]{2,1,0:T(8,128)(2,1)S(1)}, bf16[2,1024,128]{2,1,0:T(8,128)(2,1)S(1)}, u32[]{:S(2)}, u32[]{:S(2)}) %collective-permute-start.2) | collective-permute-done | bytes 524320 | tf_op jit(solution)/shard_map/ppermute | solution.py:17
  283.2 0.4 fusion.138
  283.6 0.4 fusion.140
  284.1 2.8 fusion.1
  286.9 0.7 fusion.106
  287.5 4.6 %fusion.18 = (f32[1024]{0:T(1024)S(1)}, f32[1024]{0:T(1024)S(1)}, f32[1024]{0:T(1024)S(1)}, f32[1024]{0:T(1024)S(1)}, f32[1024]{0:T(1024)S(1)}, /*index=5*/f32[1024]{0:T(1024)S(1)}, f32[1024]{0:T(1024)S(1)}, f32[1024]{0:T(1024)S(1)}) fusion(f32[1024,512]{0,1:T(8,128)S(1)} %get-tuple-element.63, f32[1024]{0:T(1024)S(1)} %maximum_maximum_fusion.1, ...), kind=kLoop, calls=%fused_computation.50 | loop fusion | flops 20963328 | bytes 16834560 | tf_op jit(solution)/shard_map/reduce_sum | solution.py:66
  292.2 0.7 convolution_add_fusion.7
  292.9 0.7 fusion.104
  293.6 0.7 fusion.102
  294.2 0.7 fusion.100
  294.9 0.7 fusion.48
  295.7 0.7 fusion.49
  296.4 0.7 fusion.57
  297.1 0.9 copy.37
  298.0 1.5 fusion.137
  299.4 1.3 fusion.139
  300.8 5.0 %fusion.9 = (f32[1024]{0:T(1024)S(1)}, f32[1024]{0:T(1024)S(1)}, f32[1024]{0:T(1024)S(1)}, f32[1024]{0:T(1024)S(1)}, f32[1024]{0:T(1024)S(1)}, /*index=5*/f32[10...) fusion(s32[1024]{0:T(1024)S(1)} %bitcast.165, s32[512]{0:T(512)S(1)} %get-tuple-element.53, ...), kind=kOutput, calls=%fused_computation.41 | convolution fusion | flops 150986752 | bytes 17223680 | tf_op jit(solution)/shard_map/dot_general | solution.py:51
  305.8 0.7 fusion.98
  306.5 0.9 copy-done.5
  307.4 4.8 %fusion.34 = (f32[1024]{0:T(1024)S(1)}, f32[1024]{0:T(1024)S(1)}, f32[1024]{0:T(1024)S(1)}, f32[1024]{0:T(1024)S(1)}, f32[1024]{0:T(1024)S(1)}, /*index=5*/f32[1024]{0:T(1024)S(1)}, f32[1024]{0:T(1024)S(1)}, f32[1024]{0:T(1024)S(1)}) fusion(f32[1024,512]{0,1:T(8,128)S(1)} %get-tuple-element.62, f32[1024]{0:T(1024)S(1)} %maximum_maximum_fusion, ...), kind=kLoop, calls=%fused_computation.66 | loop fusion | flops 20963328 | bytes 16834560 | tf_op jit(solution)/shard_map/reduce_sum | solution.py:66
  312.2 0.7 convolution_add_fusion.3
  312.9 0.3 copy-done.8
  313.2 0.7 fusion.96
  313.9 0.7 fusion.94
  314.7 0.3 copy-done.12
  315.0 0.7 fusion.92
  315.7 0.7 fusion.52
  316.4 0.7 fusion.53
  317.1 0.7 fusion.56
  317.8 0.1 copy.40
  318.1 0.2 copy.41
  318.3 15.7 %all_to_all.58 = bf16[8,128,256]{2,1,0:T(8,128)(2,1)S(1)} all-to-all(bf16[8,128,256]{2,1,0:T(8,128)(2,1)S(1)} %bitcast.151), channel_id=1, replica_groups=mesh['dp'=2,'ulysses'=8,'blk'=16] {'ulysses'}, dimensions={0} | all-to-all | bytes 1048576 | tf_op jit(solution)/shard_map/all_to_all | solution.py:167
  334.0 0.3 copy.42
  334.3 1.0 copy.43
  (69 shorter events, 1.4 us)
Async XLA Ops:
  6.5 199.0 %copy-start = (bf16[1,128,4096]{2,1,0:T(8,128)(2,1)S(1)}, bf16[1,128,4096]{2,1,0:T(8,128)(2,1)}, u32[]{:S(2)}) copy-start(bf16[1,128,4096]{2,1,0:T(8,128)(2,1)} %param.5) | copy-start | bytes 3145732
  6.5 2.0 copy-start.13
  6.5 2.1 copy-start.14
  6.5 199.0 %all-gather.2.cloned.1.call-start = ((), (), s32[]{:S(2)}) async-start(), calls=%async_computation.4 | async-start | bytes 17301504 | tf_op jit(solution)/shard_map/all_gather | solution.py:97
  9.9 205.2 %all-to-all-start = ((bf16[128,8,256]{0,2,1:T(8,128)(2,1)}), bf16[128,8,256]{0,2,1:T(8,128)(2,1)S(1)}, u32[]{:S(2)}, u32[]{:S(2)}) async-start(bf16[128,8,256]{0,2,1:T(8,128)(2,1)} %bitcast.2), calls=%async_computation | async-start | bytes 1048576 | tf_op jit(solution)/shard_map/all_to_all | solution.py:106
  215.0 11.6 %all-to-all-start.1 = ((bf16[128,8,128]{2,0,1:T(8,128)(2,1)}), bf16[128,8,128]{2,0,1:T(8,128)(2,1)S(1)}, u32[]{:S(2)}, u32[]{:S(2)}) async-start(bf16[128,8,128]{2,0,1:T(8,128)(2,1)} %pad_maximum_fusion.3), calls=%async_computation.1 | async-start | bytes 524288 | tf_op jit(solution)/shard_map/all_to_all | solution.py:107
  226.6 10.9 %all-to-all-start.2 = ((bf16[128,8,128]{2,0,1:T(8,128)(2,1)}), bf16[128,8,128]{2,0,1:T(8,128)(2,1)S(1)}, u32[]{:S(2)}, u32[]{:S(2)}) async-start(bf16[128,8,128]{2,0,1:T(8,128)(2,1)} %copy_bitcast_fusion), calls=%async_computation.2 | async-start | bytes 524288 | tf_op jit(solution)/shard_map/all_to_all | solution.py:108
  237.5 16.1 %collective-permute-start = (bf16[2,1024,128]{2,1,0:T(8,128)(2,1)S(1)}, bf16[2,1024,128]{2,1,0:T(8,128)(2,1)S(1)}, u32[]{:S(2)}, u32[]{:S(2)}) collective-permute-start(bf16[2,1024,128]{2,1,0:T(8,128)(2,1)S(1)} %pad_maximum_fusion.1), channel_id=1, source_target_pairs={{15,0},{0,1},{1,2},{2,3},{3,4},{4,5},{5,6},{6,7},{7,8},{8,9},{9,10... | collective-permute-start | bytes 1572872 | tf_op jit(solution)/shard_map/ppermute | solution.py:17
  253.6 41.3 %copy-start.7 = (bf16[2,1024,128]{2,1,0:T(8,128)(2,1)}, bf16[2,1024,128]{2,1,0:T(8,128)(2,1)S(1)}, u32[]{:S(2)}) copy-start(bf16[2,1024,128]{2,1,0:T(8,128)(2,1)S(1)} %collective-permute-done) | copy-start | bytes 1572868
  253.6 15.2 %collective-permute-start.1 = (bf16[2,1024,128]{2,1,0:T(8,128)(2,1)S(1)}, bf16[2,1024,128]{2,1,0:T(8,128)(2,1)S(1)}, u32[]{:S(2)}, u32[]{:S(2)}) collective-permute-start(bf16[2,1024,128]{2,1,0:T(8,128)(2,1)S(1)} %collective-permute-done), channel_id=1, source_target_pairs={{15,0},{0,1},{1,2},{2,3},{3,4},{4,5},{5,6},{6,7},{7,8},{8,9},{9,10... | collective-permute-start | bytes 1572872 | tf_op jit(solution)/shard_map/ppermute | solution.py:17
  268.8 26.8 %copy-start.9 = (bf16[2,1024,128]{2,1,0:T(8,128)(2,1)}, bf16[2,1024,128]{2,1,0:T(8,128)(2,1)S(1)}, u32[]{:S(2)}) copy-start(bf16[2,1024,128]{2,1,0:T(8,128)(2,1)S(1)} %collective-permute-done.1) | copy-start | bytes 1572868
  268.8 14.3 %collective-permute-start.2 = (bf16[2,1024,128]{2,1,0:T(8,128)(2,1)S(1)}, bf16[2,1024,128]{2,1,0:T(8,128)(2,1)S(1)}, u32[]{:S(2)}, u32[]{:S(2)}) collective-permute-start(bf16[2,1024,128]{2,1,0:T(8,128)(2,1)S(1)} %collective-permute-done.1), channel_id=1, source_target_pairs={{15,0},{0,1},{1,2},{2,3},{3,4},{4,5},{5,6},{6,7},{7,8},{8,9},{9,10... | collective-permute-start | bytes 1572872 | tf_op jit(solution)/shard_map/ppermute | solution.py:17
  283.2 13.2 %copy-start.11 = (bf16[2,1024,128]{2,1,0:T(8,128)(2,1)}, bf16[2,1024,128]{2,1,0:T(8,128)(2,1)S(1)}, u32[]{:S(2)}) copy-start(bf16[2,1024,128]{2,1,0:T(8,128)(2,1)S(1)} %collective-permute-done.2) | copy-start | bytes 1572868
  297.9 2.8 copy-start.2
  297.9 2.8 copy-start.3
  300.8 5.0 %copy-start.4 = (f32[1024,512]{0,1:T(8,128)S(1)}, f32[1024,512]{0,1:T(8,128)}, u32[]{:S(2)}) copy-start(f32[1024,512]{0,1:T(8,128)} %fusion.125) | copy-start | bytes 6291460
  305.8 1.6 copy-start.5
  312.2 1.0 copy-start.8
  312.9 1.1 copy-start.10
  313.9 1.0 copy-start.12
  317.0 1.0 copy-start.6
  318.0 17.3 %copy-start.1 = (bf16[1,128,4096]{2,1,0:T(8,128)(2,1)S(1)}, bf16[1,128,4096]{2,1,0:T(8,128)(2,1)}, u32[]{:S(2)}) copy-start(bf16[1,128,4096]{2,1,0:T(8,128)(2,1)} %param.5) | copy-start | bytes 3145732
Sparse Core Ops, SparseCore 0:
  9.1 196.3 all-gather.1
where the time goes:
time: 343 us; the launch traced here: 342 us
  waiting for transfers between devices  237 us (69%)
  matrix products  40.2 us (12%)
  starting transfers between devices  16.1 us (5%)
  blocking collectives  15.7 us (5%)
  between operations  14 us (4%)
  other arithmetic  12.2 us (4%)
  local copies, waits for them, and re-layouts  7.27 us (2%)
    all_gather x1, waiting for transfers between devices, shards(): lax.all_gather(pair_weight, ('dp', 'blk'), axis=0, tiled=True)  188 us
    ppermute x3, waiting for transfers between devices, from_behind(): return lax.ppermute(block, axis, route)  35.9 us
    dot_general x16, matrix products, tile_scores(): lax.dot_general(query_rows, key_rows, (((1,), (1,)), ((), ())), preferred...  21.1 us
    all_to_all x1, blocking collectives, shards(): lax.all_to_all(block_output, 'ulysses', split_axis=0, concat_axis=1, tile...  15.7 us
    dot_general x16, matrix products, add_tile(): jnp.dot(weights.astype(jnp.bfloat16), value_rows, preferred_element_type=...  11 us
    reduce_sum x2, other arithmetic, add_tile(): denominator = denominator + jnp.sum(weights, axis=1)  9.41 us
    dot_general x1, matrix products, shards(): jnp.dot(inputs_local, lax.all_gather(pair_weight, ('dp', 'blk'), axis=0,...  8.1 us
  transfers between devices with their start and end apart: 7, of which 6 were waited for; matrix products, arithmetic and copies ran while one was open for 7% of the time, Pallas kernels for 0%

commit v1 on v0

--- a/solution.py
+++ b/solution.py
@@ -94,7 +94,12 @@
     rotated_queries = rotated_queries.astype(jnp.bfloat16).reshape(token_rows, QH * HD)
     projected = jnp.dot(
         inputs_local,
-        lax.all_gather(pair_weight, ("dp", "blk"), axis=0, tiled=True),
+        jnp.concatenate(
+            lax.all_to_all(
+                jnp.stack([pair_weight] * lax.axis_size(("dp", "blk"))), ("dp", "blk"), 0, 0
+            ),
+            axis=0,
+        ),
         preferred_element_type=jnp.float32,
     )
     token_keys = rotate(

time: 343 us -> 550 us (1.60)
  waiting for transfers between devices: 237 us -> 440 us
  between operations: 14 us -> 0.64 us
  starting transfers between devices: 16.1 us -> 27.4 us
  local copies, waits for them, and re-layouts: 7.27 us -> 13.1 us
    all_to_all x0 -> x1, waiting for transfers between devices: none -> 392 us  [shards(): lax.all_to_all(jnp.stack([pair_weight] * lax.axis_size(('dp', 'blk'))), (...]
    all_gather x1 -> x0, waiting for transfers between devices: 188 us -> none  [shards(): lax.all_gather(pair_weight, ('dp', 'blk'), axis=0, tiled=True)]
    all_to_all x0 -> x1, starting transfers between devices: none -> 12.3 us  [shards(): lax.all_to_all(jnp.stack([pair_weight] * lax.axis_size(('dp', 'blk'))), (...]
    another operation x0 -> x1, local copies, waits for them, and re-layouts: none -> 6.88 us  [shards(): jnp.stack([pair_weight] * lax.axis_size(('dp', 'blk')))]
  transfers between devices with their start and end apart: 7 -> 7, of which waited for: 6 -> 6; matrix products, arithmetic and copies ran while one was open for 7% -> 4% of each run, Pallas kernels for 0% -> 0%
where the time goes in v1:
time: 550 us; the launch traced here: 549 us
  waiting for transfers between devices  440 us (80%)
  matrix products  40.2 us (7%)
  starting transfers between devices  27.4 us (5%)
  blocking collectives  15.7 us (3%)
  local copies, waits for them, and re-layouts  13.1 us (2%)
  other arithmetic  12.2 us (2%)
    all_to_all x1, waiting for transfers between devices, shards(): lax.all_to_all(jnp.stack([pair_weight] * lax.axis_size(('dp', 'blk'))), (...  392 us
    ppermute x3, waiting for transfers between devices, from_behind(): return lax.ppermute(block, axis, route)  35.9 us
    dot_general x16, matrix products, tile_scores(): lax.dot_general(query_rows, key_rows, (((1,), (1,)), ((), ())), preferred...  21.1 us
    all_to_all x1, blocking collectives, shards(): lax.all_to_all(block_output, 'ulysses', split_axis=0, concat_axis=1, tile...  15.7 us
    all_to_all x1, starting transfers between devices, shards(): lax.all_to_all(jnp.stack([pair_weight] * lax.axis_size(('dp', 'blk'))), (...  12.3 us
  transfers between devices with their start and end apart: 7, of which 6 were waited for; matrix products, arithmetic and copies ran while one was open for 4% of the time, Pallas kernels for 0%

profile of v1, /device:TPU:1, one launch (start us, length us, event | category | flops | bytes accessed | tf_op | source)
XLA Modules:
  0.0 549.1 jit_solution(13541874149968024617)
XLA Ops:
  0.0 6.9 %stack.8 = bf16[32,128,2048]{2,1,0:T(8,128)(2,1)} broadcast(bf16[128,2048]{1,0:T(8,128)(2,1)} %param.7), dimensions={1,2} | broadcast | bytes 17301504 | tf_op jit(solution)/shard_map/stack | solution.py:99
  6.9 12.3 %all-to-all-start.1 = ((bf16[32,128,2048]{2,1,0:T(8,128)(2,1)}), bf16[32,128,2048]{2,1,0:T(8,128)(2,1)}, u32[]{:S(2)}, u32[]{:S(2)}) async-start(bf16[32,128,2048]{2,1,0:T(8,128)(2,1)} %stack.8), calls=%async_computation.1 | async-start | bytes 33554432 | tf_op jit(solution)/shard_map/all_to_all | solution.py:98
  19.4 0.2 select_reduce_fusion.4
  19.7 0.2 multiply_cosine_fusion
  20.2 0.2 copy.29
  20.4 0.2 subtract_convert_fusion.1
  20.5 0.8 pad_maximum_fusion
  21.5 392.4 %all-to-all-done.1 = bf16[32,128,2048]{2,1,0:T(8,128)(2,1)} async-done(((bf16[32,128,2048]{2,1,0:T(8,128)(2,1)}), bf16[32,128,2048]{2,1,0:T(8,128)(2,1)}, u32[]{:S(2)}, u32[]{:S(2)}) %all-to-all-start.1) | async-done | bytes 16777248 | tf_op jit(solution)/shard_map/all_to_all | solution.py:98
  413.9 5.8 %all-to-all-start = ((bf16[128,8,256]{0,2,1:T(8,128)(2,1)}), bf16[128,8,256]{0,2,1:T(8,128)(2,1)S(1)}, u32[]{:S(2)}, u32[]{:S(2)}) async-start(bf16[128,8,256]{0,2,1:T(8,128)(2,1)} %bitcast.2), calls=%async_computation | async-start | bytes 1048576 | tf_op jit(solution)/shard_map/all_to_all | solution.py:111
  419.7 8.1 %fusion.58 = f32[128,2048]{1,0:T(8,128)S(1)} fusion(bf16[4096,2048]{1,0:T(8,128)(2,1)} %bitcast.7, bf16[1,128,4096]{2,1,0:T(8,128)(2,1)S(1)} %copy-done), kind=kOutput, calls=%fused_computation.98 | convolution fusion | flops 2147483648 | bytes 18874368 | tf_op jit(solution)/shard_map/dot_general | solution.py:95
  427.9 0.2 fusion.206
  428.1 0.2 subtract_convert_fusion
  428.4 0.8 pad_maximum_fusion.3
  429.2 4.8 all-to-all-start.2
  434.0 0.7 copy_bitcast_fusion
  434.7 5.7 %all-to-all-done.2 = bf16[128,8,128]{2,0,1:T(8,128)(2,1)S(1)} async-done(((bf16[128,8,128]{2,0,1:T(8,128)(2,1)}), bf16[128,8,128]{2,0,1:T(8,128)(2,1)S(1)}, u32[]{:S(2)}, u32[]{:S(2)}) %all-to-all-start.2) | async-done | bytes 262176 | tf_op jit(solution)/shard_map/all_to_all | solution.py:112
  440.5 4.4 all-to-all-start.3
  444.9 0.1 copy.30
  445.4 5.9 %all-to-all-done.3 = bf16[128,8,128]{2,0,1:T(8,128)(2,1)S(1)} async-done(((bf16[128,8,128]{2,0,1:T(8,128)(2,1)}), bf16[128,8,128]{2,0,1:T(8,128)(2,1)S(1)}, u32[]{:S(2)}, u32[]{:S(2)}) %all-to-all-start.3) | async-done | bytes 262176 | tf_op jit(solution)/shard_map/all_to_all | solution.py:113
  451.5 0.4 fusion.126
  451.9 1.8 fusion.125
  453.7 13.8 %collective-permute-done = bf16[2,1024,128]{2,1,0:T(8,128)(2,1)S(1)} collective-permute-done((bf16[2,1024,128]{2,1,0:T(8,128)(2,1)S(1)}, bf16[2,1024,128]{2,1,0:T(8,128)(2,1)S(1)}, u32[]{:S(2)}, u32[]{:S(2)}) %collective-permute-start) | collective-permute-done | bytes 524320 | tf_op jit(solution)/shard_map/ppermute | solution.py:17
  467.5 0.4 fusion.130
  468.0 0.4 fusion.132
  468.4 1.7 fusion.131
  470.1 0.4 fusion.129
  470.6 12.2 %collective-permute-done.1 = bf16[2,1024,128]{2,1,0:T(8,128)(2,1)S(1)} collective-permute-done((bf16[2,1024,128]{2,1,0:T(8,128)(2,1)S(1)}, bf16[2,1024,128]{2,1,0:T(8,128)(2,1)S(1)}, u32[]{:S(2)}, u32[]{:S(2)}) %collective-permute-start.1) | collective-permute-done | bytes 524320 | tf_op jit(solution)/shard_map/ppermute | solution.py:17
  482.7 0.4 fusion.134
  483.2 0.4 fusion.136
  483.6 1.8 fusion.133
  485.4 1.8 fusion.135
  487.1 9.9 %collective-permute-done.2 = bf16[2,1024,128]{2,1,0:T(8,128)(2,1)S(1)} collective-permute-done((bf16[2,1024,128]{2,1,0:T(8,128)(2,1)S(1)}, bf16[2,1024,128]{2,1,0:T(8,128)(2,1)S(1)}, u32[]{:S(2)}, u32[]{:S(2)}) %collective-permute-start.2) | collective-permute-done | bytes 524320 | tf_op jit(solution)/shard_map/ppermute | solution.py:17
  497.1 0.4 fusion.138
  497.5 0.4 fusion.140
  497.9 2.8 fusion.1
  500.7 0.7 fusion.106
  501.4 4.6 fusion.18
  506.0 0.7 convolution_add_fusion.7
  506.8 0.7 fusion.104
  507.4 0.7 fusion.102
  508.1 0.7 fusion.100
  508.8 0.7 fusion.48
  509.5 0.7 fusion.49
  510.2 0.7 fusion.57
  511.0 0.9 copy.37
  511.8 1.5 fusion.137
  513.3 1.3 fusion.139
  514.7 5.0 fusion.9
  519.7 0.7 fusion.98
  520.4 0.9 copy-done.5
  521.2 4.8 fusion.34
  526.0 0.7 convolution_add_fusion.3
  526.8 0.3 copy-done.9
  527.1 0.7 fusion.96
  527.8 0.7 fusion.94
  528.5 0.3 copy-done.13
  528.9 0.7 fusion.92
  529.5 0.7 fusion.52
  530.2 0.7 fusion.53
  530.9 0.7 fusion.56
  531.9 0.2 copy.41
  532.1 15.7 %all_to_all.63 = bf16[8,128,256]{2,1,0:T(8,128)(2,1)S(1)} all-to-all(bf16[8,128,256]{2,1,0:T(8,128)(2,1)S(1)} %bitcast.152), channel_id=1, replica_groups=mesh['dp'=2,'ulysses'=8,'blk'=16] {'ulysses'}, dimensions={0} | all-to-all | bytes 1048576 | tf_op jit(solution)/shard_map/all_to_all | solution.py:172
  547.9 0.3 copy.42
  548.1 1.0 copy.43
  (71 shorter events, 1.6 us)
Async XLA Ops:
  0.0 419.7 %copy-start = (bf16[1,128,4096]{2,1,0:T(8,128)(2,1)S(1)}, bf16[1,128,4096]{2,1,0:T(8,128)(2,1)}, u32[]{:S(2)}) copy-start(bf16[1,128,4096]{2,1,0:T(8,128)(2,1)} %param.5) | copy-start | bytes 3145732
  6.9 12.5 %copy-start.14 = (s32[1,32]{1,0:T(1,128)S(1)}, s32[1,32]{1,0:T(1,128)}, u32[]{:S(2)}) copy-start(s32[1,32]{1,0:T(1,128)} %param.8) | copy-start | bytes 388
  6.9 12.8 %copy-start.15 = (s32[64]{0:T(128)S(1)}, s32[64]{0:T(128)}, u32[]{:S(2)}) copy-start(s32[64]{0:T(128)} %param.9) | copy-start | bytes 772
  6.9 13.3 %copy-start.7 = (bf16[1,128,2048]{2,1,0:T(8,128)(2,1)S(1)}, bf16[1,128,2048]{2,1,0:T(8,128)(2,1)}, u32[]{:S(2)}) copy-start(bf16[1,128,2048]{2,1,0:T(8,128)(2,1)} %param.6) | copy-start | bytes 1572868
  6.9 407.0 %all-to-all-start.1 = ((bf16[32,128,2048]{2,1,0:T(8,128)(2,1)}), bf16[32,128,2048]{2,1,0:T(8,128)(2,1)}, u32[]{:S(2)}, u32[]{:S(2)}) async-start(bf16[32,128,2048]{2,1,0:T(8,128)(2,1)} %stack.8), calls=%async_computation.1 | async-start | bytes 33554432 | tf_op jit(solution)/shard_map/all_to_all | solution.py:98
  413.9 15.3 %all-to-all-start = ((bf16[128,8,256]{0,2,1:T(8,128)(2,1)}), bf16[128,8,256]{0,2,1:T(8,128)(2,1)S(1)}, u32[]{:S(2)}, u32[]{:S(2)}) async-start(bf16[128,8,256]{0,2,1:T(8,128)(2,1)} %bitcast.2), calls=%async_computation | async-start | bytes 1048576 | tf_op jit(solution)/shard_map/all_to_all | solution.py:111
  429.2 11.3 %all-to-all-start.2 = ((bf16[128,8,128]{2,0,1:T(8,128)(2,1)}), bf16[128,8,128]{2,0,1:T(8,128)(2,1)S(1)}, u32[]{:S(2)}, u32[]{:S(2)}) async-start(bf16[128,8,128]{2,0,1:T(8,128)(2,1)} %pad_maximum_fusion.3), calls=%async_computation.2 | async-start | bytes 524288 | tf_op jit(solution)/shard_map/all_to_all | solution.py:112
  440.5 10.9 %all-to-all-start.3 = ((bf16[128,8,128]{2,0,1:T(8,128)(2,1)}), bf16[128,8,128]{2,0,1:T(8,128)(2,1)S(1)}, u32[]{:S(2)}, u32[]{:S(2)}) async-start(bf16[128,8,128]{2,0,1:T(8,128)(2,1)} %copy_bitcast_fusion), calls=%async_computation.3 | async-start | bytes 524288 | tf_op jit(solution)/shard_map/all_to_all | solution.py:113
  451.4 16.1 %collective-permute-start = (bf16[2,1024,128]{2,1,0:T(8,128)(2,1)S(1)}, bf16[2,1024,128]{2,1,0:T(8,128)(2,1)S(1)}, u32[]{:S(2)}, u32[]{:S(2)}) collective-permute-start(bf16[2,1024,128]{2,1,0:T(8,128)(2,1)S(1)} %pad_maximum_fusion.1), channel_id=1, source_target_pairs={{15,0},{0,1},{1,2},{2,3},{3,4},{4,5},{5,6},{6,7},{7,8},{8,9},{9,10... | collective-permute-start | bytes 1572872 | tf_op jit(solution)/shard_map/ppermute | solution.py:17
  467.5 41.3 %copy-start.8 = (bf16[2,1024,128]{2,1,0:T(8,128)(2,1)}, bf16[2,1024,128]{2,1,0:T(8,128)(2,1)S(1)}, u32[]{:S(2)}) copy-start(bf16[2,1024,128]{2,1,0:T(8,128)(2,1)S(1)} %collective-permute-done) | copy-start | bytes 1572868
  467.5 15.2 %collective-permute-start.1 = (bf16[2,1024,128]{2,1,0:T(8,128)(2,1)S(1)}, bf16[2,1024,128]{2,1,0:T(8,128)(2,1)S(1)}, u32[]{:S(2)}, u32[]{:S(2)}) collective-permute-start(bf16[2,1024,128]{2,1,0:T(8,128)(2,1)S(1)} %collective-permute-done), channel_id=1, source_target_pairs={{15,0},{0,1},{1,2},{2,3},{3,4},{4,5},{5,6},{6,7},{7,8},{8,9},{9,10... | collective-permute-start | bytes 1572872 | tf_op jit(solution)/shard_map/ppermute | solution.py:17
  482.7 26.8 %copy-start.10 = (bf16[2,1024,128]{2,1,0:T(8,128)(2,1)}, bf16[2,1024,128]{2,1,0:T(8,128)(2,1)S(1)}, u32[]{:S(2)}) copy-start(bf16[2,1024,128]{2,1,0:T(8,128)(2,1)S(1)} %collective-permute-done.1) | copy-start | bytes 1572868
  482.7 14.3 %collective-permute-start.2 = (bf16[2,1024,128]{2,1,0:T(8,128)(2,1)S(1)}, bf16[2,1024,128]{2,1,0:T(8,128)(2,1)S(1)}, u32[]{:S(2)}, u32[]{:S(2)}) collective-permute-start(bf16[2,1024,128]{2,1,0:T(8,128)(2,1)S(1)} %collective-permute-done.1), channel_id=1, source_target_pairs={{15,0},{0,1},{1,2},{2,3},{3,4},{4,5},{5,6},{6,7},{7,8},{8,9},{9,10... | collective-permute-start | bytes 1572872 | tf_op jit(solution)/shard_map/ppermute | solution.py:17
  497.1 13.2 %copy-start.12 = (bf16[2,1024,128]{2,1,0:T(8,128)(2,1)}, bf16[2,1024,128]{2,1,0:T(8,128)(2,1)S(1)}, u32[]{:S(2)}) copy-start(bf16[2,1024,128]{2,1,0:T(8,128)(2,1)S(1)} %collective-permute-done.2) | copy-start | bytes 1572868
  511.8 2.8 copy-start.2
  511.8 2.8 copy-start.3
  514.7 5.0 copy-start.4
  519.6 1.6 copy-start.5
  526.0 1.0 copy-start.9
  526.7 1.1 copy-start.11
  527.8 1.0 copy-start.13
  530.9 1.0 copy-start.6
  531.9 17.3 %copy-start.1 = (bf16[1,128,4096]{2,1,0:T(8,128)(2,1)S(1)}, bf16[1,128,4096]{2,1,0:T(8,128)(2,1)}, u32[]{:S(2)}) copy-start(bf16[1,128,4096]{2,1,0:T(8,128)(2,1)} %param.5) | copy-start | bytes 3145732
